TPU v7x, 256 devices: a whole 4x4x8 slice. The times are simulated.
256 devices in a mesh: cls: 2 (over y_hi), dom: 16 (over y_lo, x, core), orient: 8 (over z).
Axes of the slice: x: 4, y: 4 (y_hi: 2, y_lo: 2; y = y_hi * 2 + y_lo), z: 8, core: 2. Of those that a mesh axis runs over, the one named last changes fastest.
Arguments:
- references: bfloat16 [2, 8, 8, 32768], P(None, 'cls', None, ('dom', 'orient')), may hold values from -2 to 2
- images: bfloat16 [2, 2048, 32768], P(None, ('dom', 'orient')), may hold values from -16 to 16
- orient_lists: int32 [2048, 1], P(('dom', 'orient')), may hold values from 0 to 7; in each aligned block of 16 rows (0 to 15, 16 to 31, ...) at most 3 rows name the same one
- shift_ids: int32 [2048, 1], P(('dom', 'orient')), may hold values from 0 to 63
- fixed_weights: float32 [2048, 1], P(('dom', 'orient')), may hold values from 0.2 to 2
Outputs:
- class_prob: float32 [2048, 8], P(('dom', 'orient'), 'cls')
- volume: float32 [2, 8, 8, 32768], P(None, 'cls', 'orient', 'dom')
Inputs may be any that keep to these rules, and one draw needn't show every extreme that they name: `orient_lists`: within the rows of one device (16 particles), no orientation bin is listed by more than 3 particles, a bound that some block reaches.
All inputs are finite; a program needn't handle non-finite values.
Results may differ from a plain program's by a relative error of at most 0.02.
Values may be sent and summed in bfloat16 or wider, within the bound.
A program may use at most 320 MiB of HBM per device.

v0:
```python
import math
import jax
import jax.numpy as jnp
from jax import lax
from jax.sharding import PartitionSpec as P

IMG = 256
TX = 8
TY = 8
TWO_PI = 2.0 * math.pi


def offsets(number):
    return (jnp.arange(number, dtype=jnp.int32) - number // 2).astype(jnp.float32)


def local(references, images, orient_lists, shift_ids, fixed_weights):
    here = images.shape[1]
    classes, orients = (references.shape[1], references.shape[2])
    doms = lax.axis_size("dom")
    band = images.shape[2] // doms
    particles = here * doms
    held = lax.all_to_all(images, "dom", split_axis=2, concat_axis=1, tiled=True)
    piece = lax.all_gather(references, "orient", axis=3, tiled=True)
    ids = lax.all_gather(
        jnp.concatenate([orient_lists, shift_ids], axis=1), "dom", axis=0, tiled=True
    )
    orient_ids, shift_index = (ids[:, 0], ids[:, 1])
    columns = jnp.arange(band, dtype=jnp.int32) + lax.axis_index("dom") * band
    freq_x = (columns % IMG - IMG // 2).astype(jnp.float32)
    freq_y = (columns // IMG).astype(jnp.float32)
    angle_x = TWO_PI / IMG * (offsets(TX)[:, None] * freq_x[None, :])
    angle_y = TWO_PI / IMG * (offsets(TY)[:, None] * freq_y[None, :])
    cx, sx, cy, sy = (jnp.cos(angle_x), jnp.sin(angle_x), jnp.cos(angle_y), jnp.sin(angle_y))
    re, im = (held[0].astype(jnp.float32), held[1].astype(jnp.float32))
    x_re = (re[:, None] * cx - im[:, None] * sx).astype(jnp.bfloat16).reshape(particles * TX, band)
    x_im = (re[:, None] * sx + im[:, None] * cx).astype(jnp.bfloat16).reshape(particles * TX, band)
    r_re = piece[0].reshape(classes * orients, band).astype(jnp.float32)
    r_im = piece[1].reshape(classes * orients, band).astype(jnp.float32)
    s_re = (r_re[None] * cy[:, None] + r_im[None] * sy[:, None]).astype(jnp.bfloat16)
    s_im = (r_im[None] * cy[:, None] - r_re[None] * sy[:, None]).astype(jnp.bfloat16)
    s_re = s_re.reshape(TY * classes * orients, band)
    s_im = s_im.reshape(TY * classes * orients, band)
    part = jnp.einsum("aj,bj->ab", x_re, s_re, preferred_element_type=jnp.float32)
    part = part + jnp.einsum("aj,bj->ab", x_im, s_im, preferred_element_type=jnp.float32)
    part = lax.all_to_all(
        part.reshape(doms, here * TX, -1), "dom", split_axis=0, concat_axis=0, tiled=True
    )
    logits = jnp.sum(part, axis=0).reshape(here, TX, TY, classes, orients)
    top = jnp.max(logits, axis=(1, 2, 3, 4))
    top = lax.pmax(top, "cls")
    exponent = jnp.exp(logits - top[:, None, None, None, None])
    sums = jnp.sum(exponent, axis=(1, 2, 4))
    totals = lax.psum(jnp.sum(sums, axis=1), "cls")
    class_prob = sums / totals[:, None]
    weight = (fixed_weights * class_prob).astype(jnp.bfloat16)
    weight = lax.all_gather(weight, "dom", axis=0, tiled=True)
    entry_x = (shift_index % TX - TX // 2).astype(jnp.float32)
    entry_y = (shift_index // TX - TY // 2).astype(jnp.float32)
    angle = TWO_PI / IMG * (entry_x[:, None] * freq_x[None] + entry_y[:, None] * freq_y[None])
    cosine, sine = (jnp.cos(angle), jnp.sin(angle))
    row_re = (re * cosine - im * sine).astype(jnp.bfloat16)
    row_im = (re * sine + im * cosine).astype(jnp.bfloat16)
    onehot = (orient_ids[:, None] == jnp.arange(orients, dtype=jnp.int32)[None]).astype(
        jnp.bfloat16
    )
    mixing = (onehot[:, :, None] * weight[:, None, :]).reshape(particles, orients * classes)
    grown = [
        jnp.einsum("pm,pj->mj", mixing, row, preferred_element_type=jnp.float32).reshape(
            orients, 1, classes, band
        )
        for row in (row_re, row_im)
    ]
    grown = jnp.concatenate(grown, axis=1)
    grown = lax.all_to_all(grown, "orient", split_axis=0, concat_axis=0, tiled=True)
    volume = jnp.sum(grown, axis=0)[:, :, None, :]
    return (class_prob, volume)


def solution(mesh):
    in_specs = (
        P(None, "cls", None, ("dom", "orient")),
        P(None, ("dom", "orient"), None),
        P(("dom", "orient"), None),
        P(("dom", "orient"), None),
        P(("dom", "orient"), None),
    )
    out_specs = (P(("dom", "orient"), "cls"), P(None, "cls", "orient", "dom"))
    return jax.shard_map(local, mesh=mesh, in_specs=in_specs, out_specs=out_specs, check_vma=False)
```

profile of v0, /device:TPU:1, one launch (start us, length us, event | category | flops | bytes accessed | tf_op | source)
XLA Modules:
  0.0 253.7 jit_solution(4576734842398924274)
XLA Ops:
  0.6 30.9 %copy.31 = bf16[2,16,32768]{1,0,2:T(2,128)(2,1)} copy(bf16[2,16,32768]{2,1,0:T(8,128)(2,1)} %param.6) | data formatting | bytes 4194304 | tf_op args[1]
  31.5 20.8 %reshape.408 = bf16[16,2,32768]{2,1,0:T(2,128)(2,1)} reshape(bf16[32768,2,16]{2,1,0:T(2,128)(2,1)} %bitcast.57) | data formatting | bytes 4194304
  52.3 7.0 %all-to-all-start = ((bf16[16,2,32768]{2,1,0:T(2,128)(2,1)}), bf16[16,2,32768]{2,1,0:T(2,128)(2,1)S(1)}, u32[]{:S(2)}, u32[]{:S(2)}) async-start(bf16[16,2,32768]{2,1,0:T(2,128)(2,1)} %reshape.408), calls=%async_computation | async-start | bytes 4194304 | tf_op jit(solution)/shard_map/all_to_all | solution.py:23
  59.3 24.1 %all_gather.9 = bf16[2,4,8,2048]{3,2,1,0:T(8,128)(2,1)S(1)} all-gather(bf16[2,4,8,256]{3,2,1,0:T(8,128)(2,1)S(1)} %copy-done.1), channel_id=1, replica_groups=mesh['cls'=2,'dom'=16,'orient'=8] {'orient'}, dimensions={3}, use_global_device_ids=true | all-gather | bytes 294912 | tf_op jit(solution)/shard_map/all_gather | solution.py:24
  83.5 0.5 fusion.24
  84.0 1.5 subtract_convert_fusion.2
  85.6 1.3 all-to-all-done
  86.9 14.4 %reshape.409 = bf16[32768,2,16]{2,1,0:T(2,128)(2,1)} reshape(bf16[16,2,32768]{2,1,0:T(2,128)(2,1)S(1)} %all-to-all-done) | data formatting | bytes 4194304
  101.3 23.3 %copy.45 = bf16[2,16,16,2048]{3,2,1,0:T(8,128)(2,1)S(1)} copy(bf16[2,16,16,2048]{1,0,3,2:T(2,128)(2,1)} %bitcast.56) | data formatting | bytes 4194304 | tf_op jit(solution)/shard_map/all_to_all | solution.py:23
  124.6 0.5 slice_convert_fusion.1
  125.2 1.2 copy.33
  126.4 1.2 copy.34
  127.6 2.8 %fusion.1 = f32[2048,256]{1,0:T(8,128)S(1)} fusion(bf16[256,2048]{1,0:T(8,128)(2,1)S(1)} %bitcast.68, f32[8,2048]{1,0:T(8,128)S(1)} %get-tuple-element.15, f32[256,2048]{1,0:T(8,128)S(1)} %bitcast.65, f32[8,2048]{1,0:T(8,128)S(1)} %get-tuple-element.14, f32[256,2048]{1,0:T(8,128)S(1)} %bitcast.63), kind=kOutput, calls=%fused_computation.3 | convolution fusion | flops 2164260864 | bytes 7471104 | tf_op jit(solution)/shard_map/aj,bj->ab/dot_general | solution.py:44
  130.4 3.9 %fusion.14 = f32[2048,256]{1,0:T(8,128)} fusion(f32[2048,256]{1,0:T(8,128)S(1)} %fusion.1, bf16[256,2048]{1,0:T(8,128)(2,1)S(1)} %bitcast.67, f32[8,2048]{1,0:T(8,128)S(1)} %get-tuple-element.15, f32[256,2048]{1,0:T(8,128)S(1)} %bitcast.66, f32[8,2048]{1,0:T(8,128)S(1)} %get-tuple-element.14, f32[256,2048]{1,0:T(8,128)S(1)} %bitcast.64), kind=kOutput, calls=%fused_computation.14 | convolution fusion | flops 2164785152 | bytes 9568256 | tf_op jit(solution)/shard_map/aj,bj->ab/dot_general | solution.py:45
  134.3 8.8 %all-to-all-start.1 = ((f32[16,128,256]{2,1,0:T(8,128)}), f32[16,128,256]{2,1,0:T(8,128)}, u32[]{:S(2)}, u32[]{:S(2)}) async-start(f32[16,128,256]{2,1,0:T(8,128)} %bitcast.62), calls=%async_computation.1 | async-start | bytes 4194304 | tf_op jit(solution)/shard_map/all_to_all | solution.py:46
  143.1 40.1 %all-gather = s32[16,16,2]{1,2,0:T(2,128)S(1)} all-gather(s32[1,16,2]{1,2,0:T(2,128)S(1)} %add_bitcast_fusion), channel_id=1, replica_groups=mesh['cls'=2,'dom'=16,'orient'=8] {'dom'}, dimensions={0}, use_global_device_ids=true | all-gather | bytes 2176 | tf_op jit(solution)/shard_map/all_gather | solution.py:25
  183.3 0.1 reshape.391
  183.4 0.1 mul.358
  183.5 0.1 copy.38
  183.5 0.1 mul.362
  183.6 0.1 copy.39
  183.7 8.7 %subtract_convert_fusion.1 = (bf16[1,16,16,2048]{3,1,2,0:T(8,128)(2,1)S(1)}, bf16[1,16,16,2048]{3,1,2,0:T(8,128)(2,1)S(1)}) fusion(f32[2048]{0:T(1024)S(1)} %get-tuple-element.23, f32[16,16]{0,1:T(8,128)S(1)} %copy.39, f32[2048]{0:T(1024)S(1)} %get-tuple-element.22, f32[16,16]{0,1:T(8,128)S(1)} %copy.38, bf16[2,16,16,2048]{3,1,2,0:T(8,128)(2,1)S(1)} %bitcast.59), kind=kLoop, calls=%fused_computation.18 | loop fusion | flops 7340032 | bytes 4212736 | tf_op jit(solution)/shard_map/convert_element_type | solution.py:62
  192.4 0.6 copy.40
  193.0 1.6 copy.42
  194.6 0.0 all-to-all-done.1
  194.6 1.7 reduce_sum.43
  196.3 0.1 copy.35
  196.4 0.1 reduce_max.10
  196.5 0.1 reduce_max.14
  196.6 0.1 reduce_max.18
  196.7 5.3 %pmax.7 = f32[16]{0:T(128)S(1)} all-reduce(f32[16]{0:T(128)S(1)} %reduce_max.18), channel_id=1, replica_groups=mesh['cls'=2,'dom'=16,'orient'=8] {'cls'}, use_global_device_ids=true, to_apply=%region_3.4 | all-reduce | flops 16 | bytes 128 | tf_op jit(solution)/shard_map/pmax | solution.py:51
  202.0 0.1 sub.78
  202.1 0.1 sub.79
  202.2 0.2 exponential_reduce_fusion.1
  202.4 0.1 reduce_sum.46
  202.5 0.1 reduce_sum.47
  202.6 5.3 %psum.7 = f32[16]{0:T(128)S(1)} all-reduce(f32[16]{0:T(128)S(1)} %reduce_sum.47), channel_id=1, replica_groups=mesh['cls'=2,'dom'=16,'orient'=8] {'cls'}, use_global_device_ids=true, to_apply=%region_7.8 | all-reduce | flops 16 | bytes 128 | tf_op jit(solution)/shard_map/psum | solution.py:54
  207.9 1.1 reshape.384
  209.0 0.5 exponential_reduce_fusion
  209.5 0.6 fusion.36
  210.1 18.2 %all-gather.1 = bf16[16,16,4]{1,2,0:T(4,128)(2,1)S(1)} all-gather(bf16[1,16,4]{1,2,0:T(4,128)(2,1)S(1)} %get-tuple-element.4), channel_id=1, replica_groups=mesh['cls'=2,'dom'=16,'orient'=8] {'dom'}, dimensions={0}, use_global_device_ids=true | all-gather | bytes 2176 | tf_op jit(solution)/shard_map/all_gather | solution.py:57
  228.4 0.1 reshape.393
  228.6 0.3 convolution_bitcast_fusion.1
  228.8 1.5 convolution_bitcast_fusion
  230.4 0.3 copy.44
  230.7 22.2 %all_to_all.25 = f32[8,2,4,2048]{3,2,1,0:T(4,128)S(1)} all-to-all(f32[8,2,4,2048]{3,2,1,0:T(4,128)S(1)} %copy.44), channel_id=1, replica_groups=mesh['cls'=2,'dom'=16,'orient'=8] {'orient'}, dimensions={0} | all-to-all | bytes 1048576 | tf_op jit(solution)/shard_map/all_to_all | solution.py:75
  253.0 0.1 reduce_sum.48
  253.1 0.7 broadcast_in_dim.2
  (23 shorter events, 0.2 us)
Async XLA Ops:
  52.3 7.0 %copy-start.1 = (bf16[2,4,8,256]{3,2,1,0:T(8,128)(2,1)S(1)}, bf16[2,4,8,256]{3,2,1,0:T(8,128)(2,1)}, u32[]{:S(2)}) copy-start(bf16[2,4,8,256]{3,2,1,0:T(8,128)(2,1)} %param.5) | copy-start | bytes 98308
  52.3 34.6 %all-to-all-start = ((bf16[16,2,32768]{2,1,0:T(2,128)(2,1)}), bf16[16,2,32768]{2,1,0:T(2,128)(2,1)S(1)}, u32[]{:S(2)}, u32[]{:S(2)}) async-start(bf16[16,2,32768]{2,1,0:T(2,128)(2,1)} %reshape.408), calls=%async_computation | async-start | bytes 4194304 | tf_op jit(solution)/shard_map/all_to_all | solution.py:23
  126.4 1.2 copy-start
  134.3 8.8 %copy-start.3 = (s32[16,1]{0,1:T(1,128)S(1)}, s32[16,1]{0,1:T(1,128)}, u32[]{:S(2)}) copy-start(s32[16,1]{0,1:T(1,128)} %param.8) | copy-start | bytes 196
  134.3 8.8 %copy-start.4 = (s32[16,1]{0,1:T(1,128)S(1)}, s32[16,1]{0,1:T(1,128)}, u32[]{:S(2)}) copy-start(s32[16,1]{0,1:T(1,128)} %param.7) | copy-start | bytes 196
  134.3 60.3 %all-to-all-start.1 = ((f32[16,128,256]{2,1,0:T(8,128)}), f32[16,128,256]{2,1,0:T(8,128)}, u32[]{:S(2)}, u32[]{:S(2)}) async-start(f32[16,128,256]{2,1,0:T(8,128)} %bitcast.62), calls=%async_computation.1 | async-start | bytes 4194304 | tf_op jit(solution)/shard_map/all_to_all | solution.py:46
  207.9 1.6 copy-start.2
where the time goes:
time: 258 us; the launch traced here: 254 us
  blocking collectives  115 us (45%)
  local copies, waits for them, and re-layouts  97 us (38%)
  starting transfers between devices  15.7 us (6%)
  other arithmetic  15 us (6%)
  matrix products  8.47 us (3%)
    unnamed x15, local copies, waits for them, and re-layouts  66.2 us
    all_gather x1, blocking collectives, local(): lax.all_gather(jnp.concatenate([orient_lists, shift_ids], axis=1), 'dom',...  40.1 us
    all_gather x1, blocking collectives, local(): piece = lax.all_gather(references, 'orient', axis=3, tiled=True)  24.1 us
    all_to_all x1, local copies, waits for them, and re-layouts, local(): lax.all_to_all(images, 'dom', split_axis=2, concat_axis=1, tiled=True)  23.3 us
    all_to_all x1, blocking collectives, local(): lax.all_to_all(grown, 'orient', split_axis=0, concat_axis=0, tiled=True)  22.2 us
    all_gather x1, blocking collectives, local(): weight = lax.all_gather(weight, 'dom', axis=0, tiled=True)  18.2 us
    all_to_all x1, starting transfers between devices, local(): lax.all_to_all(part.reshape(doms, here * TX, -1), 'dom', split_axis=0, co...  8.77 us
    convert_element_type x1, other arithmetic, local(): row_re = (re * cosine - im * sine).astype(jnp.bfloat16)  8.74 us
  transfers between devices with their start and end apart: 2, of which 1 were waited for; matrix products, arithmetic and copies ran while one was open for 5% of the time, Pallas kernels for 0%

commit v1 on v0

--- a/solution.py
+++ b/solution.py
@@ -20,7 +20,11 @@
     doms = lax.axis_size("dom")
     band = images.shape[2] // doms
     particles = here * doms
-    held = lax.all_to_all(images, "dom", split_axis=2, concat_axis=1, tiled=True)
+    far_arr = lax.axis_size("dom")
+    x_new = jnp.split(images, far_arr, axis=2)
+    current_block = jnp.stack(x_new)
+    tile_out = lax.all_to_all(current_block, axis_name="dom", split_axis=0, concat_axis=0)
+    held = jnp.concatenate(tile_out, 1)
     piece = lax.all_gather(references, "orient", axis=3, tiled=True)
     ids = lax.all_gather(
         jnp.concatenate([orient_lists, shift_ids], axis=1), "dom", axis=0, tiled=True

time: 258 us -> 187 us (0.72); the launches traced: 254 us -> 186 us
  local copies, waits for them, and re-layouts: 97 us -> 28.6 us
    unnamed x15 -> x27, local copies, waits for them, and re-layouts: 66.2 us -> 24.3 us
    all_to_all x1 -> x0, local copies, waits for them, and re-layouts: 23.3 us -> none  [local(): lax.all_to_all(images, 'dom', split_axis=2, concat_axis=1, tiled=True)]
    convert_element_type x4 -> x0, local copies, waits for them, and re-layouts: 4.57 us -> none  [the longest x2 2.44 us: local(): re, im = (held[0].astype(jnp.float32), held[1].astype(jnp.float32))]
  transfers between devices with their start and end apart: 2 -> 2, of which waited for: 1 -> 1; matrix products, arithmetic and copies ran while one was open for 5% -> 6% of each run, Pallas kernels for 0% -> 0%
where the time goes in v1:
time: 187 us; the launch traced here: 186 us
  blocking collectives  115 us (61%)
  local copies, waits for them, and re-layouts  28.6 us (15%)
  other arithmetic  15.9 us (9%)
  starting transfers between devices  15.7 us (8%)
  matrix products  8.48 us (5%)
    all_gather x1, blocking collectives, local(): lax.all_gather(jnp.concatenate([orient_lists, shift_ids], axis=1), 'dom',...  40.1 us
    unnamed x27, local copies, waits for them, and re-layouts  24.3 us
    all_gather x1, blocking collectives, local(): piece = lax.all_gather(references, 'orient', axis=3, tiled=True)  24.1 us
    all_to_all x1, blocking collectives, local(): lax.all_to_all(grown, 'orient', split_axis=0, concat_axis=0, tiled=True)  22.2 us
    all_gather x1, blocking collectives, local(): weight = lax.all_gather(weight, 'dom', axis=0, tiled=True)  18.2 us
    convert_element_type x1, other arithmetic, local(): row_re = (re * cosine - im * sine).astype(jnp.bfloat16)  9.62 us
    all_to_all x1, starting transfers between devices, local(): lax.all_to_all(part.reshape(doms, here * TX, -1), 'dom', split_axis=0, co...  8.75 us
    all_to_all x1, starting transfers between devices, local(): lax.all_to_all(current_block, axis_name='dom', split_axis=0, concat_axis=0)  6.96 us
  transfers between devices with their start and end apart: 2, of which 1 were waited for; matrix products, arithmetic and copies ran while one was open for 6% of the time, Pallas kernels for 0%

profile of v1, /device:TPU:1, one launch (start us, length us, event | category | flops | bytes accessed | tf_op | source)
XLA Modules:
  0.0 186.2 jit_solution(8441519617908995131)
XLA Ops:
  0.6 1.6 bitcast_dynamic-update-slice_fusion.15
  2.2 1.6 bitcast_dynamic-update-slice_fusion.14
  3.7 1.6 bitcast_dynamic-update-slice_fusion.13
  5.3 1.6 bitcast_dynamic-update-slice_fusion.12
  6.9 1.6 bitcast_dynamic-update-slice_fusion.11
  8.4 1.5 bitcast_dynamic-update-slice_fusion.10
  10.0 1.6 bitcast_dynamic-update-slice_fusion.9
  11.6 1.6 bitcast_dynamic-update-slice_fusion.8
  13.1 1.6 bitcast_dynamic-update-slice_fusion.7
  14.7 1.6 bitcast_dynamic-update-slice_fusion.6
  16.3 1.6 bitcast_dynamic-update-slice_fusion.5
  17.8 1.6 bitcast_dynamic-update-slice_fusion.4
  19.4 1.6 bitcast_dynamic-update-slice_fusion.3
  20.9 1.6 bitcast_dynamic-update-slice_fusion.2
  22.5 1.6 bitcast_dynamic-update-slice_fusion.1
  24.0 1.6 bitcast_dynamic-update-slice_fusion
  25.6 7.0 %all-to-all-start = ((bf16[16,2,16,2048]{3,2,1,0:T(8,128)(2,1)}), bf16[16,2,16,2048]{3,2,1,0:T(8,128)(2,1)S(1)}, u32[]{:S(2)}, u32[]{:S(2)}) async-start(bf16[16,2,16,2048]{3,2,1,0:T(8,128)(2,1)} %bitcast_dynamic-update-slice_fusion), calls=%async_computation | async-start | bytes 4194304 | tf_op jit(solution)/shard_map/all_to_all | solution.py:26
  32.6 24.1 %all_gather.9 = bf16[2,4,8,2048]{3,2,1,0:T(8,128)(2,1)S(1)} all-gather(bf16[2,4,8,256]{3,2,1,0:T(8,128)(2,1)S(1)} %copy-done.1), channel_id=1, replica_groups=mesh['cls'=2,'dom'=16,'orient'=8] {'orient'}, dimensions={3}, use_global_device_ids=true | all-gather | bytes 294912 | tf_op jit(solution)/shard_map/all_gather | solution.py:28
  56.8 0.5 fusion.24
  57.3 1.5 subtract_convert_fusion.2
  58.9 1.4 all-to-all-done
  60.2 0.5 slice_convert_fusion.1
  60.8 0.7 copy-done
  61.5 2.8 %fusion.1 = f32[2048,256]{1,0:T(8,128)S(1)} fusion(bf16[256,2048]{1,0:T(8,128)(2,1)S(1)} %bitcast.95, f32[8,2048]{1,0:T(8,128)S(1)} %get-tuple-element.15, f32[256,2048]{1,0:T(8,128)S(1)} %bitcast.91, f32[8,2048]{1,0:T(8,128)S(1)} %get-tuple-element.14, f32[256,2048]{1,0:T(8,128)S(1)} %bitcast.89), kind=kOutput, calls=%fused_computation.3 | convolution fusion | flops 2164260864 | bytes 7471104 | tf_op jit(solution)/shard_map/aj,bj->ab/dot_general | solution.py:48
  64.2 3.9 %fusion.14 = f32[2048,256]{1,0:T(8,128)} fusion(f32[2048,256]{1,0:T(8,128)S(1)} %fusion.1, bf16[256,2048]{1,0:T(8,128)(2,1)S(1)} %bitcast.94, f32[8,2048]{1,0:T(8,128)S(1)} %get-tuple-element.15, f32[256,2048]{1,0:T(8,128)S(1)} %bitcast.92, f32[8,2048]{1,0:T(8,128)S(1)} %get-tuple-element.14, f32[256,2048]{1,0:T(8,128)S(1)} %bitcast.90), kind=kOutput, calls=%fused_computation.14 | convolution fusion | flops 2164785152 | bytes 9568256 | tf_op jit(solution)/shard_map/aj,bj->ab/dot_general | solution.py:49
  68.2 8.8 %all-to-all-start.1 = ((f32[16,128,256]{2,1,0:T(8,128)}), f32[16,128,256]{2,1,0:T(8,128)}, u32[]{:S(2)}, u32[]{:S(2)}) async-start(f32[16,128,256]{2,1,0:T(8,128)} %bitcast.93), calls=%async_computation.1 | async-start | bytes 4194304 | tf_op jit(solution)/shard_map/all_to_all | solution.py:50
  77.0 40.1 %all-gather = s32[16,16,2]{1,2,0:T(2,128)S(1)} all-gather(s32[1,16,2]{1,2,0:T(2,128)S(1)} %add_bitcast_fusion), channel_id=1, replica_groups=mesh['cls'=2,'dom'=16,'orient'=8] {'dom'}, dimensions={0}, use_global_device_ids=true | all-gather | bytes 2176 | tf_op jit(solution)/shard_map/all_gather | solution.py:29
  117.4 9.6 %subtract_convert_fusion.1 = (bf16[1,16,16,2048]{3,2,0,1:T(8,128)(2,1)S(1)}, bf16[1,16,16,2048]{3,2,0,1:T(8,128)(2,1)}) fusion(f32[2048]{0:T(1024)S(1)} %get-tuple-element.23, f32[16,16]{1,0:T(8,128)S(1)} %mul.362, f32[2048]{0:T(1024)S(1)} %get-tuple-element.22, f32[16,16]{1,0:T(8,128)S(1)} %mul.358, bf16[2,16,16,2048]{3,2,0,1:T(8,128)(2,1)S(1)} %bitcast.86), kind=kLoop, calls=%fused_computation.18 | loop fusion | flops 7340032 | bytes 4212736 | tf_op jit(solution)/shard_map/convert_element_type | solution.py:66
  127.0 1.7 reduce_sum.43
  128.7 0.1 copy.11
  128.8 0.1 reduce_max.10
  129.0 0.1 reduce_max.18
  129.2 5.3 %pmax.7 = f32[16]{0:T(128)S(1)} all-reduce(f32[16]{0:T(128)S(1)} %reduce_max.18), channel_id=1, replica_groups=mesh['cls'=2,'dom'=16,'orient'=8] {'cls'}, use_global_device_ids=true, to_apply=%region_3.4 | all-reduce | flops 16 | bytes 128 | tf_op jit(solution)/shard_map/pmax | solution.py:55
  134.5 0.1 sub.79
  134.6 0.2 exponential_reduce_fusion.1
  134.9 0.1 reduce_sum.47
  135.0 5.3 %psum.7 = f32[16]{0:T(128)S(1)} all-reduce(f32[16]{0:T(128)S(1)} %reduce_sum.47), channel_id=1, replica_groups=mesh['cls'=2,'dom'=16,'orient'=8] {'cls'}, use_global_device_ids=true, to_apply=%region_7.8 | all-reduce | flops 16 | bytes 128 | tf_op jit(solution)/shard_map/psum | solution.py:58
  140.3 1.1 reshape.389
  141.5 0.5 exponential_reduce_fusion
  142.0 0.6 fusion.36
  142.6 18.2 %all-gather.1 = bf16[16,16,4]{1,2,0:T(4,128)(2,1)S(1)} all-gather(bf16[1,16,4]{1,2,0:T(4,128)(2,1)S(1)} %get-tuple-element.4), channel_id=1, replica_groups=mesh['cls'=2,'dom'=16,'orient'=8] {'dom'}, dimensions={0}, use_global_device_ids=true | all-gather | bytes 2176 | tf_op jit(solution)/shard_map/all_gather | solution.py:61
  160.8 0.1 reshape.398
  161.0 1.5 convolution_bitcast_fusion
  162.5 0.3 convolution_bitcast_fusion.1
  162.8 0.3 copy.16
  163.2 22.2 %all_to_all.15 = f32[8,2,4,2048]{3,2,1,0:T(4,128)S(1)} all-to-all(f32[8,2,4,2048]{3,2,1,0:T(4,128)S(1)} %copy.16), channel_id=1, replica_groups=mesh['cls'=2,'dom'=16,'orient'=8] {'orient'}, dimensions={0} | all-to-all | bytes 1048576 | tf_op jit(solution)/shard_map/all_to_all | solution.py:79
  185.4 0.1 reduce_sum.48
  185.5 0.7 broadcast_in_dim.2
  (29 shorter events, 0.7 us)
Async XLA Ops:
  25.6 7.0 %copy-start.1 = (bf16[2,4,8,256]{3,2,1,0:T(8,128)(2,1)S(1)}, bf16[2,4,8,256]{3,2,1,0:T(8,128)(2,1)}, u32[]{:S(2)}) copy-start(bf16[2,4,8,256]{3,2,1,0:T(8,128)(2,1)} %param.5) | copy-start | bytes 98308
  25.6 34.6 %all-to-all-start = ((bf16[16,2,16,2048]{3,2,1,0:T(8,128)(2,1)}), bf16[16,2,16,2048]{3,2,1,0:T(8,128)(2,1)S(1)}, u32[]{:S(2)}, u32[]{:S(2)}) async-start(bf16[16,2,16,2048]{3,2,1,0:T(8,128)(2,1)} %bitcast_dynamic-update-slice_fusion), calls=%async_computation | async-start | bytes 4194304 | tf_op jit(solution)/shard_map/all_to_all | solution.py:26
  60.2 1.2 copy-start
  68.2 8.8 %copy-start.3 = (s32[16,1]{0,1:T(1,128)S(1)}, s32[16,1]{0,1:T(1,128)}, u32[]{:S(2)}) copy-start(s32[16,1]{0,1:T(1,128)} %param.8) | copy-start | bytes 196
  68.2 8.8 %copy-start.4 = (s32[16,1]{0,1:T(1,128)S(1)}, s32[16,1]{0,1:T(1,128)}, u32[]{:S(2)}) copy-start(s32[16,1]{0,1:T(1,128)} %param.7) | copy-start | bytes 196
  68.2 58.8 %all-to-all-start.1 = ((f32[16,128,256]{2,1,0:T(8,128)}), f32[16,128,256]{2,1,0:T(8,128)}, u32[]{:S(2)}, u32[]{:S(2)}) async-start(f32[16,128,256]{2,1,0:T(8,128)} %bitcast.93), calls=%async_computation.1 | async-start | bytes 4194304 | tf_op jit(solution)/shard_map/all_to_all | solution.py:50
  140.3 1.6 copy-start.2
